TPU v7x, 32 devices: a whole 2x2x4 slice. The times are simulated.
32 devices in a mesh: dp: 4 (over x, core), expert: 8 (over z, y).
Axes of the slice: x: 2, y: 2, z: 4, core: 2. Of those that a mesh axis runs over, the one named last changes fastest.
Arguments:
- x_online: bfloat16 [4096, 2048], P(('dp', 'expert')), may hold values from -6 to 6
- x_target: bfloat16 [4096, 2048], P(('dp', 'expert')), may hold values from -6 to 6
- routes: int32 [4096, 2], P(('dp', 'expert')), may hold values from 0 to 15, all different within a row; in each aligned block of 128 rows (0 to 127, 128 to 255, ...) at most 32 rows name the same one
- gate_probs: float32 [4096, 2], P(('dp', 'expert')), may hold values from 0.2 to 1
- expert_place: int32 [16], replicated, may hold values from 0 to 15, each once
- gate_online: bfloat16 [32, 2048, 256], P(('dp', 'expert')), may hold values from -0.125 to 0.125
- up_online: bfloat16 [32, 2048, 256], P(('dp', 'expert')), may hold values from -0.125 to 0.125
- down_online: bfloat16 [32, 256, 2048], P(('dp', 'expert')), may hold values from -0.25 to 0.25
- gate_target: bfloat16 [32, 2048, 256], P(('dp', 'expert')), may hold values from -0.125 to 0.125
- up_target: bfloat16 [32, 2048, 256], P(('dp', 'expert')), may hold values from -0.125 to 0.125
- down_target: bfloat16 [32, 256, 2048], P(('dp', 'expert')), may hold values from -0.25 to 0.25
Outputs:
- input_grad: bfloat16 [4096, 2048], P(('dp', 'expert'))
- grad_gate: bfloat16 [32, 2048, 256], P(('dp', 'expert'))
- grad_up: bfloat16 [32, 2048, 256], P(('dp', 'expert'))
- grad_down: bfloat16 [32, 256, 2048], P(('dp', 'expert'))
Inputs may be any that keep to these rules, and one draw needn't show every extreme that they name: `routes`: each row names two different experts. Among the 128 rows of one device no expert is named more than 32 times, and in every draw some expert is named exactly 32 times by the rows of some device. `expert_place`: A permutation: each expert has a place of its own.
All inputs are finite; a program needn't handle non-finite values.
Results may differ from a plain program's by a relative error of at most 0.011.
Values may be sent and summed in bfloat16 or wider, within the bound.
A program may use at most 128 MiB of HBM per device.

v0:
```python
import jax
import jax.numpy as jnp
from jax import lax
from jax.sharding import PartitionSpec as P

contract_last = (((1,), (1,)), ((), ()))
contract_first = (((0,), (0,)), ((), ()))


def swapped(block, axis, bit):
    count = lax.axis_size(axis)
    route = []
    for low in range(count):
        high = low | 1 << bit
        if high != low and high < count:
            route += [(low, high), (high, low)]
    return lax.ppermute(block, axis, route)


def hidden_forward(inputs, w_gate, w_up):
    pre_gate = jnp.dot(inputs, w_gate, preferred_element_type=jnp.float32)
    pre_up = jnp.dot(inputs, w_up, preferred_element_type=jnp.float32)
    hidden = (jax.nn.silu(pre_gate) * pre_up).astype(jnp.bfloat16)
    return (pre_gate, pre_up, hidden)


def hidden_grads(cotangent, pre_gate, pre_up, w_down):
    d_hidden = lax.dot_general(cotangent, w_down, contract_last, preferred_element_type=jnp.float32)
    sigmoid_gate = jax.nn.sigmoid(pre_gate)
    d_gate = (d_hidden * pre_up * sigmoid_gate * (1.0 + pre_gate * (1.0 - sigmoid_gate))).astype(
        jnp.bfloat16
    )
    d_up = (d_hidden * jax.nn.silu(pre_gate)).astype(jnp.bfloat16)
    return (d_gate, d_up)


def input_rows(d_gate, d_up, w_gate, w_up):
    total = lax.dot_general(d_gate, w_gate, contract_last, preferred_element_type=jnp.float32)
    total = total + lax.dot_general(d_up, w_up, contract_last, preferred_element_type=jnp.float32)
    return total.astype(jnp.bfloat16)


def outer_sum(left, right):
    return lax.dot_general(left, right, contract_first, preferred_element_type=jnp.float32)


def shards(
    x_online,
    x_target,
    routes,
    gate_probs,
    expert_place,
    gate_online,
    up_online,
    down_online,
    gate_target,
    up_target,
    down_target,
):
    tok_rows, model_width = x_online.shape
    dp_count = lax.axis_size("dp")
    expert_count = lax.axis_size("expert")
    unit_count = dp_count * expert_count
    experts = expert_place.shape[0]
    capacity = 2 * ((2 * tok_rows + experts - 1) // experts)
    half_cap = capacity // 2
    half_width = gate_online.shape[2]
    chosen = routes.reshape(-1)
    onehot = (chosen[:, None] == jnp.arange(experts, dtype=jnp.int32)[None, :]).astype(jnp.int32)
    before = jnp.cumsum(onehot, axis=0) - onehot
    position = jnp.sum(before * onehot, axis=1)
    slot_place = jnp.sum(onehot * expert_place[None, :], axis=1)
    flat_slot = (2 * slot_place + position // half_cap) * half_cap + position % half_cap
    owner_token = jnp.arange(2 * tok_rows, dtype=jnp.int32) // 2

    def to_units(source):
        blank_rows = jnp.zeros((unit_count * half_cap, model_width), source.dtype)
        return (
            blank_rows.at[flat_slot]
            .set(source)
            .reshape(dp_count, expert_count, half_cap, model_width)
        )

    def from_units(block):
        picked = block.reshape(unit_count * half_cap, model_width)[flat_slot]
        return picked.astype(jnp.float32).reshape(tok_rows, 2, model_width)

    partner = swapped(
        (gate_online, up_online, down_online, gate_target, up_target, down_target), "expert", 0
    )
    gate_full = jnp.concatenate([gate_online[0], partner[0][0]], axis=1)
    up_full = jnp.concatenate([up_online[0], partner[1][0]], axis=1)
    down_full = jnp.concatenate([down_online[0], partner[2][0]], axis=0)
    gate_tfull = jnp.concatenate([gate_target[0], partner[3][0]], axis=1)
    up_tfull = jnp.concatenate([up_target[0], partner[4][0]], axis=1)
    down_tfull = jnp.concatenate([down_target[0], partner[5][0]], axis=0)
    recv_online, recv_target = (
        lax.all_to_all(
            lax.all_to_all(
                to_units(x_online[owner_token]), "dp", split_axis=0, concat_axis=0, tiled=True
            ),
            "expert",
            split_axis=1,
            concat_axis=1,
            tiled=True,
        ),
        lax.all_to_all(
            lax.all_to_all(
                to_units(x_target[owner_token]), "dp", split_axis=0, concat_axis=0, tiled=True
            ),
            "expert",
            split_axis=1,
            concat_axis=1,
            tiled=True,
        ),
    )
    unit_shape = recv_online.shape
    inputs_online = recv_online.reshape(-1, model_width)
    inputs_target = recv_target.reshape(-1, model_width)
    pre_gate, pre_up, hidden = hidden_forward(inputs_online, gate_full, up_full)
    out_online = jnp.dot(hidden, down_full, preferred_element_type=jnp.float32).astype(jnp.bfloat16)
    hidden_target = hidden_forward(inputs_target, gate_tfull, up_tfull)[2]
    out_target = jnp.dot(hidden_target, down_tfull, preferred_element_type=jnp.float32).astype(
        jnp.bfloat16
    )
    back_online, back_target = (
        lax.all_to_all(
            lax.all_to_all(
                out_online.reshape(unit_shape), "dp", split_axis=0, concat_axis=0, tiled=True
            ),
            "expert",
            split_axis=1,
            concat_axis=1,
            tiled=True,
        ),
        lax.all_to_all(
            lax.all_to_all(
                out_target.reshape(unit_shape), "dp", split_axis=0, concat_axis=0, tiled=True
            ),
            "expert",
            split_axis=1,
            concat_axis=1,
            tiled=True,
        ),
    )
    y_online = jnp.sum(from_units(back_online) * gate_probs[:, :, None], axis=1)
    y_target = jnp.sum(from_units(back_target) * gate_probs[:, :, None], axis=1)
    cotangent = (
        (gate_probs[:, :, None] * (y_online - y_target)[:, None, :])
        .astype(jnp.bfloat16)
        .reshape(2 * tok_rows, model_width)
    )
    cot_recv = lax.all_to_all(
        lax.all_to_all(to_units(cotangent), "dp", split_axis=0, concat_axis=0, tiled=True),
        "expert",
        split_axis=1,
        concat_axis=1,
        tiled=True,
    )
    cot_rows = cot_recv.reshape(-1, model_width)
    d_gate, d_up = hidden_grads(cot_rows, pre_gate, pre_up, down_full)
    d_rows = input_rows(d_gate, d_up, gate_full, up_full)
    back_grads = lax.all_to_all(
        lax.all_to_all(d_rows.reshape(unit_shape), "dp", split_axis=0, concat_axis=0, tiled=True),
        "expert",
        split_axis=1,
        concat_axis=1,
        tiled=True,
    )
    input_grad = jnp.sum(from_units(back_grads), axis=1).astype(jnp.bfloat16)
    g_gate = outer_sum(inputs_online, d_gate)
    g_up = outer_sum(inputs_online, d_up)
    g_down = outer_sum(hidden, cot_rows)
    sent = (
        swapped(g_gate[:, half_width:].astype(jnp.bfloat16), "expert", 0).astype(jnp.float32),
        swapped(g_up[:, half_width:].astype(jnp.bfloat16), "expert", 0).astype(jnp.float32),
        swapped(g_down[half_width:].astype(jnp.bfloat16), "expert", 0).astype(jnp.float32),
    )
    grad_gate = g_gate[:, :half_width] + sent[0]
    grad_up = g_up[:, :half_width] + sent[1]
    grad_down = g_down[:half_width] + sent[2]
    return (
        input_grad,
        grad_gate.astype(jnp.bfloat16)[None],
        grad_up.astype(jnp.bfloat16)[None],
        grad_down.astype(jnp.bfloat16)[None],
    )


def solution(mesh):
    in_specs = (
        P(("dp", "expert"), None),
        P(("dp", "expert"), None),
        P(("dp", "expert"), None),
        P(("dp", "expert"), None),
        P(),
        P(("dp", "expert"), None, None),
        P(("dp", "expert"), None, None),
        P(("dp", "expert"), None, None),
        P(("dp", "expert"), None, None),
        P(("dp", "expert"), None, None),
        P(("dp", "expert"), None, None),
    )
    out_specs = (
        P(("dp", "expert"), None),
        P(("dp", "expert"), None, None),
        P(("dp", "expert"), None, None),
        P(("dp", "expert"), None, None),
    )
    return jax.shard_map(shards, mesh=mesh, in_specs=in_specs, out_specs=out_specs, check_vma=False)
```

profile of v0, /device:TPU:0, one launch (start us, length us, event | category | flops | bytes accessed | tf_op | source)
XLA Modules:
  0.0 683.3 jit_solution(6394342232910622523)
XLA Ops:
  3.4 7.0 %scatter_custom_fusion.1 = bf16[512,2048]{1,0:T(8,128)(2,1)} fusion(s32[256]{0:T(256)S(1)} %bitcast.88, bf16[128,2048]{1,0:T(8,128)(2,1)S(1)} %copy-done, s32[1024]{0:T(1024)S(1)} %pad_clamp_fusion.1, bf16[]{:T(256)} %constant.52.clone.1), kind=kCustom, calls=%fused_computation.45 | custom fusion | bytes 2097154 | tf_op jit(solution)/shard_map/scatter | solution.py:80
  10.4 4.2 all-to-all-start.4
  14.6 7.1 %scatter_custom_fusion = bf16[512,2048]{1,0:T(8,128)(2,1)} fusion(s32[256]{0:T(256)S(1)} %bitcast.89, bf16[128,2048]{1,0:T(8,128)(2,1)} %param.11, s32[1024]{0:T(1024)S(1)} %pad_clamp_fusion.1, bf16[]{:T(256)} %constant.52.clone.1), kind=kCustom, calls=%fused_computation.47 | custom fusion | bytes 2097664 | tf_op jit(solution)/shard_map/scatter | solution.py:80
  21.8 18.6 %all-to-all-done.4 = bf16[4,8,16,2048]{3,2,1,0:T(8,128)(2,1)S(1)} async-done(((bf16[4,8,16,2048]{3,2,1,0:T(8,128)(2,1)}), bf16[4,8,16,2048]{3,2,1,0:T(8,128)(2,1)S(1)}, u32[]{:S(2)}, u32[]{:S(2)}) %all-to-all-start.4) | async-done | bytes 2097184 | tf_op jit(solution)/shard_map/all_to_all | solution.py:108
  40.3 4.7 all-to-all-start
  46.5 24.2 %all-to-all-done = bf16[4,8,16,2048]{3,2,1,0:T(8,128)(2,1)} async-done(((bf16[4,8,16,2048]{3,2,1,0:T(8,128)(2,1)}), bf16[4,8,16,2048]{3,2,1,0:T(8,128)(2,1)}, u32[]{:S(2)}, u32[]{:S(2)}) %all-to-all-start) | async-done | bytes 2097184 | tf_op jit(solution)/shard_map/all_to_all | solution.py:99
  70.8 6.7 all-to-all-start.5
  80.6 44.9 %all-to-all-done.5 = bf16[4,8,16,2048]{3,2,0,1:T(8,128)(2,1)S(1)} async-done(((bf16[4,8,16,2048]{3,2,0,1:T(8,128)(2,1)}), bf16[4,8,16,2048]{3,2,0,1:T(8,128)(2,1)S(1)}, u32[]{:S(2)}, u32[]{:S(2)}) %all-to-all-start.5) | async-done | bytes 2097184 | tf_op jit(solution)/shard_map/all_to_all | solution.py:107
  126.8 3.6 all-to-all-start.1
  138.2 40.9 %collective-permute-done.3 = bf16[1,2048,256]{2,1,0:T(8,128)(2,1)S(1)} collective-permute-done((bf16[1,2048,256]{2,1,0:T(8,128)(2,1)}, bf16[1,2048,256]{2,1,0:T(8,128)(2,1)S(1)}, u32[]{:S(2)}, u32[]{:S(2)}) %collective-permute-start.3) | collective-permute-done | bytes 1048608 | tf_op jit(solution)/shard_map/ppermute | solution.py:17
  181.4 20.2 %collective-permute-done.5 = bf16[1,256,2048]{2,1,0:T(8,128)(2,1)S(1)} collective-permute-done((bf16[1,256,2048]{2,1,0:T(8,128)(2,1)}, bf16[1,256,2048]{2,1,0:T(8,128)(2,1)S(1)}, u32[]{:S(2)}, u32[]{:S(2)}) %collective-permute-start.5) | collective-permute-done | bytes 1048608 | tf_op jit(solution)/shard_map/ppermute | solution.py:17
  202.6 21.5 %collective-permute-done.4 = bf16[1,2048,256]{2,1,0:T(8,128)(2,1)S(1)} collective-permute-done((bf16[1,2048,256]{2,1,0:T(8,128)(2,1)}, bf16[1,2048,256]{2,1,0:T(8,128)(2,1)S(1)}, u32[]{:S(2)}, u32[]{:S(2)}) %collective-permute-start.4) | collective-permute-done | bytes 1048608 | tf_op jit(solution)/shard_map/ppermute | solution.py:17
  225.0 6.8 %convolution_convert_fusion = bf16[512,2048]{1,0:T(8,128)(2,1)} fusion(bf16[256,2048]{1,0:T(8,128)(2,1)} %bitcast.102, bf16[256,2048]{1,0:T(8,128)(2,1)} %bitcast.96, f32[512,512]{1,0:T(8,128)} %fusion.3, bf16[512,2048]{1,0:T(8,128)(2,1)} %bitcast.82, bf16[2048,256]{1,0:T(8,128)(2,1)} %bitcast.103, bf16[2048,256]{1,0:T(8,128)(2,1)} %bitcast.97), kind=kOutput, calls=%fused_computation.9 | convolution fusion | flops 2158493696 | bytes 9437184 | tf_op jit(solution)/shard_map/dot_general | solution.py:123
  231.9 4.5 all-to-all-start.6
  236.6 10.0 %collective-permute-done = bf16[1,2048,256]{2,1,0:T(8,128)(2,1)} collective-permute-done((bf16[1,2048,256]{2,1,0:T(8,128)(2,1)}, bf16[1,2048,256]{2,1,0:T(8,128)(2,1)}, u32[]{:S(2)}, u32[]{:S(2)}) %collective-permute-start) | collective-permute-done | bytes 1048608 | tf_op jit(solution)/shard_map/ppermute | solution.py:17
  249.2 19.9 %collective-permute-done.1 = bf16[1,2048,256]{2,1,0:T(8,128)(2,1)} collective-permute-done((bf16[1,2048,256]{2,1,0:T(8,128)(2,1)}, bf16[1,2048,256]{2,1,0:T(8,128)(2,1)}, u32[]{:S(2)}, u32[]{:S(2)}) %collective-permute-start.1) | collective-permute-done | bytes 1048608 | tf_op jit(solution)/shard_map/ppermute | solution.py:17
  272.7 17.5 %collective-permute-done.2 = bf16[1,256,2048]{2,1,0:T(8,128)(2,1)S(1)} collective-permute-done((bf16[1,256,2048]{2,1,0:T(8,128)(2,1)}, bf16[1,256,2048]{2,1,0:T(8,128)(2,1)S(1)}, u32[]{:S(2)}, u32[]{:S(2)}) %collective-permute-start.2) | collective-permute-done | bytes 1048608 | tf_op jit(solution)/shard_map/ppermute | solution.py:17
  300.7 22.4 %all-to-all-done.2 = bf16[4,8,16,2048]{3,2,1,0:T(8,128)(2,1)S(1)} async-done(((bf16[4,8,16,2048]{3,2,1,0:T(8,128)(2,1)}), bf16[4,8,16,2048]{3,2,1,0:T(8,128)(2,1)S(1)}, u32[]{:S(2)}, u32[]{:S(2)}) %all-to-all-start.2) | async-done | bytes 2097184 | tf_op jit(solution)/shard_map/all_to_all | solution.py:128
  324.5 4.5 all-to-all-start.7
  332.2 44.9 %all-to-all-done.7 = bf16[4,8,16,2048]{3,2,0,1:T(8,128)(2,1)S(1)} async-done(((bf16[4,8,16,2048]{3,2,0,1:T(8,128)(2,1)}), bf16[4,8,16,2048]{3,2,0,1:T(8,128)(2,1)S(1)}, u32[]{:S(2)}, u32[]{:S(2)}) %all-to-all-start.7) | async-done | bytes 2097184 | tf_op jit(solution)/shard_map/all_to_all | solution.py:136
  378.5 4.8 all-to-all-start.3
  391.0 40.0 %all-to-all-done.3 = bf16[4,8,16,2048]{3,2,0,1:T(8,128)(2,1)} async-done(((bf16[4,8,16,2048]{3,2,0,1:T(8,128)(2,1)}), bf16[4,8,16,2048]{3,2,0,1:T(8,128)(2,1)}, u32[]{:S(2)}, u32[]{:S(2)}) %all-to-all-start.3) | async-done | bytes 2097184 | tf_op jit(solution)/shard_map/all_to_all | solution.py:127
  438.6 7.7 %multiply_reduce_fusion = (f32[128,2048]{1,0:T(8,128)S(1)}, f32[128,2048]{1,0:T(8,128)S(1)}) fusion(f32[128,2,2048]{2,1,0:T(2,128)S(1)} %copy-done.4, f32[128,2]{1,0:T(8,128)S(1)} %copy.52, f32[128,2,2048]{2,1,0:T(2,128)} %reshape.233), kind=kLoop, calls=%fused_computation.35 | loop fusion | flops 1572864 | bytes 6292480 | tf_op jit(solution)/shard_map/reduce_sum | solution.py:147
  451.7 3.8 scatter_custom_fusion.2
  455.4 29.3 %all_to_all.60 = bf16[4,8,16,2048]{3,2,1,0:T(8,128)(2,1)S(1)} all-to-all(bf16[4,8,16,2048]{3,2,1,0:T(8,128)(2,1)} %bitcast.75), channel_id=1, replica_groups=mesh['dp'=4,'expert'=8] {'dp'}, dimensions={0} | all-to-all | bytes 4194304 | tf_op jit(solution)/shard_map/all_to_all | solution.py:154
  485.0 51.5 %all_to_all.61 = bf16[4,8,16,2048]{3,2,0,1:T(8,128)(2,1)S(1)} all-to-all(bf16[4,8,16,2048]{3,2,0,1:T(8,128)(2,1)S(1)} %copy.62), channel_id=1, replica_groups=mesh['dp'=4,'expert'=8] {'expert'}, dimensions={1} | all-to-all | bytes 4194304 | tf_op jit(solution)/shard_map/all_to_all | solution.py:153
  546.2 28.2 %all_to_all.62 = bf16[4,8,16,2048]{3,2,1,0:T(8,128)(2,1)S(1)} all-to-all(bf16[4,8,16,2048]{3,2,1,0:T(8,128)(2,1)S(1)} %bitcast.74), channel_id=1, replica_groups=mesh['dp'=4,'expert'=8] {'dp'}, dimensions={0} | all-to-all | bytes 4194304 | tf_op jit(solution)/shard_map/all_to_all | solution.py:164
  575.9 4.5 all-to-all-start.11
  588.8 40.2 %collective-permute-done.6 = bf16[2048,256]{1,0:T(8,128)(2,1)S(1)} collective-permute-done((bf16[2048,256]{1,0:T(8,128)(2,1)S(1)}, bf16[2048,256]{1,0:T(8,128)(2,1)S(1)}, u32[]{:S(2)}, u32[]{:S(2)}) %collective-permute-start.6) | collective-permute-done | bytes 1048608 | tf_op jit(solution)/shard_map/ppermute | solution.py:17
  630.4 21.1 %collective-permute-done.7 = bf16[2048,256]{1,0:T(8,128)(2,1)S(1)} collective-permute-done((bf16[2048,256]{1,0:T(8,128)(2,1)S(1)}, bf16[2048,256]{1,0:T(8,128)(2,1)S(1)}, u32[]{:S(2)}, u32[]{:S(2)}) %collective-permute-start.7) | collective-permute-done | bytes 1048608 | tf_op jit(solution)/shard_map/ppermute | solution.py:17
  652.8 19.5 %collective-permute-done.8 = bf16[256,2048]{1,0:T(8,128)(2,1)S(1)} collective-permute-done((bf16[256,2048]{1,0:T(8,128)(2,1)S(1)}, bf16[256,2048]{1,0:T(8,128)(2,1)S(1)}, u32[]{:S(2)}, u32[]{:S(2)}) %collective-permute-start.8) | collective-permute-done | bytes 1048608 | tf_op jit(solution)/shard_map/ppermute | solution.py:17
  679.5 3.6 reduce_sum.55
  (122 shorter events, 93.6 us)
Async XLA Ops:
  10.4 29.9 %all-to-all-start.4 = ((bf16[4,8,16,2048]{3,2,1,0:T(8,128)(2,1)}), bf16[4,8,16,2048]{3,2,1,0:T(8,128)(2,1)S(1)}, u32[]{:S(2)}, u32[]{:S(2)}) async-start(bf16[4,8,16,2048]{3,2,1,0:T(8,128)(2,1)} %bitcast.79), calls=%async_computation.4 | async-start | bytes 4194304 | tf_op jit(solution)/shard_map/all_to_all | solution.py:108
  40.3 30.4 %all-to-all-start = ((bf16[4,8,16,2048]{3,2,1,0:T(8,128)(2,1)}), bf16[4,8,16,2048]{3,2,1,0:T(8,128)(2,1)}, u32[]{:S(2)}, u32[]{:S(2)}) async-start(bf16[4,8,16,2048]{3,2,1,0:T(8,128)(2,1)} %bitcast.78), calls=%async_computation | async-start | bytes 4194304 | tf_op jit(solution)/shard_map/all_to_all | solution.py:99
  70.8 54.7 %all-to-all-start.5 = ((bf16[4,8,16,2048]{3,2,0,1:T(8,128)(2,1)}), bf16[4,8,16,2048]{3,2,0,1:T(8,128)(2,1)S(1)}, u32[]{:S(2)}, u32[]{:S(2)}) async-start(bf16[4,8,16,2048]{3,2,0,1:T(8,128)(2,1)} %copy.58), calls=%async_computation.5 | async-start | bytes 4194304 | tf_op jit(solution)/shard_map/all_to_all | solution.py:107
  126.8 105.1 %all-to-all-start.1 = ((bf16[4,8,16,2048]{3,2,0,1:T(8,128)(2,1)}), bf16[4,8,16,2048]{3,2,0,1:T(8,128)(2,1)S(1)}, u32[]{:S(2)}, u32[]{:S(2)}) async-start(bf16[4,8,16,2048]{3,2,0,1:T(8,128)(2,1)} %copy.53), calls=%async_computation.1 | async-start | bytes 4194304 | tf_op jit(solution)/shard_map/all_to_all | solution.py:98
  130.4 48.7 %copy-start.18 = (bf16[1,2048,256]{2,1,0:T(8,128)(2,1)S(1)}, bf16[1,2048,256]{2,1,0:T(8,128)(2,1)}, u32[]{:S(2)}) copy-start(bf16[1,2048,256]{2,1,0:T(8,128)(2,1)} %param.19) | copy-start | bytes 3145732
  130.4 48.7 %collective-permute-start.3 = (bf16[1,2048,256]{2,1,0:T(8,128)(2,1)}, bf16[1,2048,256]{2,1,0:T(8,128)(2,1)S(1)}, u32[]{:S(2)}, u32[]{:S(2)}) collective-permute-start(bf16[1,2048,256]{2,1,0:T(8,128)(2,1)} %param.19), channel_id=1, source_target_pairs={{0,1},{1,0},{2,3},{3,2},{4,5},{5,4},{6,7},{7,6},{8,9},{9,8},{10,11... | collective-permute-start | bytes 3145736 | tf_op jit(solution)/shard_map/ppermute | solution.py:17
  132.4 69.2 %collective-permute-start.5 = (bf16[1,256,2048]{2,1,0:T(8,128)(2,1)}, bf16[1,256,2048]{2,1,0:T(8,128)(2,1)S(1)}, u32[]{:S(2)}, u32[]{:S(2)}) collective-permute-start(bf16[1,256,2048]{2,1,0:T(8,128)(2,1)} %param.21), channel_id=1, source_target_pairs={{0,1},{1,0},{2,3},{3,2},{4,5},{5,4},{6,7},{7,6},{8,9},{9,8},{10,11... | collective-permute-start | bytes 3145736 | tf_op jit(solution)/shard_map/ppermute | solution.py:17
  132.5 91.6 %collective-permute-start.4 = (bf16[1,2048,256]{2,1,0:T(8,128)(2,1)}, bf16[1,2048,256]{2,1,0:T(8,128)(2,1)S(1)}, u32[]{:S(2)}, u32[]{:S(2)}) collective-permute-start(bf16[1,2048,256]{2,1,0:T(8,128)(2,1)} %param.20), channel_id=1, source_target_pairs={{0,1},{1,0},{2,3},{3,2},{4,5},{5,4},{6,7},{7,6},{8,9},{9,8},{10,11... | collective-permute-start | bytes 3145736 | tf_op jit(solution)/shard_map/ppermute | solution.py:17
  134.5 112.2 %collective-permute-start = (bf16[1,2048,256]{2,1,0:T(8,128)(2,1)}, bf16[1,2048,256]{2,1,0:T(8,128)(2,1)}, u32[]{:S(2)}, u32[]{:S(2)}) collective-permute-start(bf16[1,2048,256]{2,1,0:T(8,128)(2,1)} %param.16), channel_id=1, source_target_pairs={{0,1},{1,0},{2,3},{3,2},{4,5},{5,4},{6,7},{7,6},{8,9},{9,8},{10,11... | collective-permute-start | bytes 3145736 | tf_op jit(solution)/shard_map/ppermute | solution.py:17
  134.5 134.6 %collective-permute-start.1 = (bf16[1,2048,256]{2,1,0:T(8,128)(2,1)}, bf16[1,2048,256]{2,1,0:T(8,128)(2,1)}, u32[]{:S(2)}, u32[]{:S(2)}) collective-permute-start(bf16[1,2048,256]{2,1,0:T(8,128)(2,1)} %param.17), channel_id=1, source_target_pairs={{0,1},{1,0},{2,3},{3,2},{4,5},{5,4},{6,7},{7,6},{8,9},{9,8},{10,11... | collective-permute-start | bytes 3145736 | tf_op jit(solution)/shard_map/ppermute | solution.py:17
  138.2 43.1 %copy-start.10 = (bf16[4,8,16,2048]{3,2,1,0:T(8,128)(2,1)}, bf16[4,8,16,2048]{3,2,1,0:T(8,128)(2,1)S(1)}, u32[]{:S(2)}) copy-start(bf16[4,8,16,2048]{3,2,1,0:T(8,128)(2,1)S(1)} %copy.59) | copy-start | bytes 6291460
  231.9 62.0 %all-to-all-start.6 = ((bf16[4,8,16,2048]{3,2,1,0:T(8,128)(2,1)}), bf16[4,8,16,2048]{3,2,1,0:T(8,128)(2,1)}, u32[]{:S(2)}, u32[]{:S(2)}) async-start(bf16[4,8,16,2048]{3,2,1,0:T(8,128)(2,1)} %bitcast.80), calls=%async_computation.6 | async-start | bytes 4194304 | tf_op jit(solution)/shard_map/all_to_all | solution.py:137
  236.3 10.3 %copy-start.11 = (bf16[1,2048,256]{2,1,0:T(8,128)(2,1)S(1)}, bf16[1,2048,256]{2,1,0:T(8,128)(2,1)}, u32[]{:S(2)}) copy-start(bf16[1,2048,256]{2,1,0:T(8,128)(2,1)} %param.16) | copy-start | bytes 3145732
  236.4 53.9 %collective-permute-start.2 = (bf16[1,256,2048]{2,1,0:T(8,128)(2,1)}, bf16[1,256,2048]{2,1,0:T(8,128)(2,1)S(1)}, u32[]{:S(2)}, u32[]{:S(2)}) collective-permute-start(bf16[1,256,2048]{2,1,0:T(8,128)(2,1)} %param.18), channel_id=1, source_target_pairs={{0,1},{1,0},{2,3},{3,2},{4,5},{5,4},{6,7},{7,6},{8,9},{9,8},{10,11... | collective-permute-start | bytes 3145736 | tf_op jit(solution)/shard_map/ppermute | solution.py:17
  236.6 32.5 %copy-start.2 = (bf16[4,8,16,2048]{3,2,1,0:T(8,128)(2,1)}, bf16[4,8,16,2048]{3,2,1,0:T(8,128)(2,1)S(1)}, u32[]{:S(2)}) copy-start(bf16[4,8,16,2048]{3,2,1,0:T(8,128)(2,1)S(1)} %copy.54) | copy-start | bytes 6291460
  246.6 22.5 %copy-start.13 = (bf16[1,2048,256]{2,1,0:T(8,128)(2,1)S(1)}, bf16[1,2048,256]{2,1,0:T(8,128)(2,1)}, u32[]{:S(2)}) copy-start(bf16[1,2048,256]{2,1,0:T(8,128)(2,1)} %param.17) | copy-start | bytes 3145732
  249.2 23.5 %copy-start.25 = (f32[512,512]{1,0:T(8,128)}, f32[512,512]{1,0:T(8,128)S(1)}, u32[]{:S(2)}) copy-start(f32[512,512]{1,0:T(8,128)S(1)} %fusion.17) | copy-start | bytes 3145732
  269.1 22.1 %copy-start.19 = (bf16[1,256,2048]{2,1,0:T(8,128)(2,1)S(1)}, bf16[1,256,2048]{2,1,0:T(8,128)(2,1)}, u32[]{:S(2)}) copy-start(bf16[1,256,2048]{2,1,0:T(8,128)(2,1)} %param.18) | copy-start | bytes 3145732
  272.7 21.2 %copy-start.15 = (bf16[512,512]{1,0:T(8,128)(2,1)}, bf16[512,512]{1,0:T(8,128)(2,1)S(1)}, u32[]{:S(2)}) copy-start(bf16[512,512]{1,0:T(8,128)(2,1)S(1)} %get-tuple-element.10) | copy-start | bytes 1572868
  293.9 29.3 %all-to-all-start.2 = ((bf16[4,8,16,2048]{3,2,1,0:T(8,128)(2,1)}), bf16[4,8,16,2048]{3,2,1,0:T(8,128)(2,1)S(1)}, u32[]{:S(2)}, u32[]{:S(2)}) async-start(bf16[4,8,16,2048]{3,2,1,0:T(8,128)(2,1)} %bitcast.83), calls=%async_computation.2 | async-start | bytes 4194304 | tf_op jit(solution)/shard_map/all_to_all | solution.py:128
  324.5 52.6 %all-to-all-start.7 = ((bf16[4,8,16,2048]{3,2,0,1:T(8,128)(2,1)}), bf16[4,8,16,2048]{3,2,0,1:T(8,128)(2,1)S(1)}, u32[]{:S(2)}, u32[]{:S(2)}) async-start(bf16[4,8,16,2048]{3,2,0,1:T(8,128)(2,1)} %copy.60), calls=%async_computation.7 | async-start | bytes 4194304 | tf_op jit(solution)/shard_map/all_to_all | solution.py:136
  332.2 51.1 %copy-start.17 = (f32[128,2]{0,1:T(2,128)S(1)}, f32[128,2]{0,1:T(2,128)}, u32[]{:S(2)}) copy-start(f32[128,2]{0,1:T(2,128)} %param.14) | copy-start | bytes 3076
  378.5 52.6 %all-to-all-start.3 = ((bf16[4,8,16,2048]{3,2,0,1:T(8,128)(2,1)}), bf16[4,8,16,2048]{3,2,0,1:T(8,128)(2,1)}, u32[]{:S(2)}, u32[]{:S(2)}) async-start(bf16[4,8,16,2048]{3,2,0,1:T(8,128)(2,1)} %copy.55), calls=%async_computation.3 | async-start | bytes 4194304 | tf_op jit(solution)/shard_map/all_to_all | solution.py:127
  435.1 3.5 copy-start.4
  536.5 2.9 copy-start.27
  536.7 4.4 copy-start.5
  575.9 4.5 copy-start.3
  575.9 97.8 %all-to-all-start.11 = ((bf16[4,8,16,2048]{3,2,0,1:T(8,128)(2,1)}), bf16[4,8,16,2048]{3,2,0,1:T(8,128)(2,1)}, u32[]{:S(2)}, u32[]{:S(2)}) async-start(bf16[4,8,16,2048]{3,2,0,1:T(8,128)(2,1)} %copy.64), calls=%async_computation.11 | async-start | bytes 4194304 | tf_op jit(solution)/shard_map/all_to_all | solution.py:163
  581.8 47.2 %collective-permute-start.6 = (bf16[2048,256]{1,0:T(8,128)(2,1)S(1)}, bf16[2048,256]{1,0:T(8,128)(2,1)S(1)}, u32[]{:S(2)}, u32[]{:S(2)}) collective-permute-start(bf16[2048,256]{1,0:T(8,128)(2,1)S(1)} %slice.77), channel_id=1, source_target_pairs={{0,1},{1,0},{2,3},{3,2},{4,5},{5,4},{6,7},{7,6},{8,9},{9,8},{10,11... | collective-permute-start | bytes 3145736 | tf_op jit(solution)/shard_map/ppermute | solution.py:17
  585.2 66.2 %collective-permute-start.7 = (bf16[2048,256]{1,0:T(8,128)(2,1)S(1)}, bf16[2048,256]{1,0:T(8,128)(2,1)S(1)}, u32[]{:S(2)}, u32[]{:S(2)}) collective-permute-start(bf16[2048,256]{1,0:T(8,128)(2,1)S(1)} %slice.76), channel_id=1, source_target_pairs={{0,1},{1,0},{2,3},{3,2},{4,5},{5,4},{6,7},{7,6},{8,9},{9,8},{10,11... | collective-permute-start | bytes 3145736 | tf_op jit(solution)/shard_map/ppermute | solution.py:17
  588.1 84.3 %collective-permute-start.8 = (bf16[256,2048]{1,0:T(8,128)(2,1)S(1)}, bf16[256,2048]{1,0:T(8,128)(2,1)S(1)}, u32[]{:S(2)}, u32[]{:S(2)}) collective-permute-start(bf16[256,2048]{1,0:T(8,128)(2,1)S(1)} %slice.75), channel_id=1, source_target_pairs={{0,1},{1,0},{2,3},{3,2},{4,5},{5,4},{6,7},{7,6},{8,9},{9,8},{10,11... | collective-permute-start | bytes 3145736 | tf_op jit(solution)/shard_map/ppermute | solution.py:17
  675.4 7.7 %copy-start.1 = (bf16[128,2048]{1,0:T(8,128)(2,1)S(1)}, bf16[128,2048]{1,0:T(8,128)(2,1)}, u32[]{:S(2)}) copy-start(bf16[128,2048]{1,0:T(8,128)(2,1)} %param.12) | copy-start | bytes 1572868
  (14 other events, 23.8 us)
where the time goes:
time: 693 us; the launch traced here: 683 us
  waiting for transfers between devices  406 us (59%)
  blocking collectives  109 us (16%)
  local copies, waits for them, and re-layouts  68.1 us (10%)
  starting transfers between devices  50 us (7%)
  matrix products  28.4 us (4%)
  other arithmetic  20.7 us (3%)
    ppermute x9, waiting for transfers between devices, swapped(): return lax.ppermute(block, axis, route)  211 us
    all_to_all x1, blocking collectives, shards(): lax.all_to_all(lax.all_to_all(to_units(cotangent), 'dp', split_axis=0, co...  51.5 us
    all_to_all x1, waiting for transfers between devices, shards(): lax.all_to_all(lax.all_to_all(out_target.reshape(unit_shape), 'dp', split...  44.9 us
    all_to_all x1, waiting for transfers between devices, shards(): lax.all_to_all(lax.all_to_all(to_units(x_target[owner_token]), 'dp', spli...  44.9 us
    all_to_all x1, waiting for transfers between devices, shards(): lax.all_to_all(lax.all_to_all(out_online.reshape(unit_shape), 'dp', split...  40 us
    all_to_all x1, blocking collectives, shards(): lax.all_to_all(to_units(cotangent), 'dp', split_axis=0, concat_axis=0, ti...  29.3 us
    all_to_all x1, blocking collectives, shards(): lax.all_to_all(d_rows.reshape(unit_shape), 'dp', split_axis=0, concat_axi...  28.2 us
    all_to_all x1, waiting for transfers between devices, shards(): lax.all_to_all(to_units(x_online[owner_token]), 'dp', split_axis=0, conca...  24.2 us
  transfers between devices with their start and end apart: 18, of which 15 were waited for; matrix products, arithmetic and copies ran while one was open for 8% of the time, Pallas kernels for 0%

commit v1 on v0

--- a/solution.py
+++ b/solution.py
@@ -1,6 +1,10 @@
+import functools
+
 import jax
 import jax.numpy as jnp
 from jax import lax
+from jax.experimental import pallas as pl
+from jax.experimental.pallas import tpu as pltpu
 from jax.sharding import PartitionSpec as P
 
 contract_last = (((1,), (1,)), ((), ()))
@@ -44,7 +48,7 @@
     return lax.dot_general(left, right, contract_first, preferred_element_type=jnp.float32)
 
 
-def shards(
+def shards_plain(
     x_online,
     x_target,
     routes,
@@ -187,6 +191,393 @@
     )
 
 
+MESH = pl.DeviceIdType.MESH
+F32 = jnp.float32
+BF16 = jnp.bfloat16
+
+
+def dot(left, right, dims=(((1,), (0,)), ((), ()))):
+    return lax.dot_general(left, right, dims, preferred_element_type=F32)
+
+
+def step_kernel(
+    slots,
+    n_ex,
+    cap,
+    flat_ref,
+    flat_t_ref,
+    probs_ref,
+    xo_ref,
+    xt_ref,
+    w0_ref,
+    w1_ref,
+    w2_ref,
+    w3_ref,
+    w4_ref,
+    w5_ref,
+    ig_ref,
+    gg_ref,
+    gu_ref,
+    gd_ref,
+    wg,
+    wu,
+    wd,
+    sx,
+    rx,
+    pd,
+    pr,
+    ret,
+    rc,
+    pre_g,
+    pre_u,
+    hid,
+    dgu,
+    w_sem,
+    send_sem,
+    recv_sem,
+    fsend_sem,
+    frecv_sem,
+    ysend_sem,
+    yrecv_sem,
+    bsend_sem,
+    brecv_sem,
+):
+    tok, width = xo_ref.shape
+    rows = slots * cap
+    half = wg.shape[2]
+    tile = 512
+    dp, ex = lax.axis_index("dp"), lax.axis_index("expert")
+    side = lax.rem(ex, 2)
+    me = lax.div(dp * n_ex + ex, 2)
+    partner = (dp, ex + 1 - 2 * side)
+
+    def peer(slot):
+        unit = 2 * slot + side
+        return (lax.div(unit, n_ex), lax.rem(unit, n_ex))
+
+    def chunk(index):
+        return pl.ds(pl.multiple_of(index * cap, cap), cap)
+
+    barrier = pltpu.get_barrier_semaphore()
+
+    def greet(o, carry):
+        pl.semaphore_signal(
+            barrier, inc=1, device_id=peer(lax.rem(me + o, slots)), device_id_type=MESH
+        )
+        return carry
+
+    lax.fori_loop(1, slots, greet, 0)
+    pl.semaphore_signal(barrier, inc=1, device_id=partner, device_id_type=MESH)
+
+    weight_copies = [
+        pltpu.make_async_copy(source, target, w_sem.at[i])
+        for i, (source, target) in enumerate(
+            [
+                (w0_ref, wg.at[0]),
+                (w1_ref, wu.at[0]),
+                (w2_ref, wd.at[0]),
+                (w3_ref, wg.at[1]),
+                (w4_ref, wu.at[1]),
+                (w5_ref, wd.at[1]),
+            ]
+        )
+    ]
+    for copy in weight_copies:
+        copy.start()
+
+    def one_hot(compare):
+        return jnp.where(compare, 1.0, 0.0).astype(BF16)
+
+    row_iota = lax.broadcasted_iota(jnp.int32, (rows, tok), 0)
+    put = [one_hot(row_iota == flat_t_ref[k : k + 1, :]) for k in range(2)]
+    put_any = one_hot((row_iota == flat_t_ref[0:1, :]) | (row_iota == flat_t_ref[1:2, :]))
+    col_iota = lax.broadcasted_iota(jnp.int32, (tok, rows), 1)
+    take = [one_hot(col_iota == flat_ref[:, k : k + 1]) for k in range(2)]
+    take_any = one_hot((col_iota == flat_ref[:, 0:1]) | (col_iota == flat_ref[:, 1:2]))
+
+    def columns(body):
+        def step(i, carry):
+            body(pl.ds(pl.multiple_of(i * tile, tile), tile))
+            return carry
+
+        lax.fori_loop(0, width // tile, step, 0)
+
+    def each(low, body):
+        def step(o, carry):
+            body(o)
+            return carry
+
+        lax.fori_loop(low, slots, step, 0)
+
+    def out_copy(net, dst, o):
+        to = lax.rem(me + o, slots)
+        return pltpu.make_async_remote_copy(
+            src_ref=sx.at[net, chunk(to)],
+            dst_ref=dst.at[0, chunk(o)],
+            send_sem=send_sem.at[net, o],
+            recv_sem=recv_sem.at[net, o],
+            device_id=peer(to),
+            device_id_type=MESH,
+        )
+
+    def fwd_copy(net, dst, o):
+        return pltpu.make_async_remote_copy(
+            src_ref=dst.at[0, chunk(o)],
+            dst_ref=dst.at[1, chunk(o)],
+            send_sem=fsend_sem.at[net, o],
+            recv_sem=frecv_sem.at[net, o],
+            device_id=partner,
+            device_id_type=MESH,
+        )
+
+    def scatter_start(net, dst):
+        each(1, lambda o: out_copy(net, dst, o).start())
+        dst[0, 0:cap] = sx[net, chunk(me)]
+        fwd_copy(net, dst, 0).start()
+
+    def relay(net, dst):
+        def body(o):
+            out_copy(net, dst, o).wait_recv()
+            fwd_copy(net, dst, o).start()
+
+        each(1, body)
+
+    def arrived(net, dst):
+        each(0, lambda o: fwd_copy(net, dst, o).wait_recv())
+
+    def scatter_end(net, dst):
+        each(0, lambda o: fwd_copy(net, dst, o).wait_send())
+        each(1, lambda o: out_copy(net, dst, o).wait_send())
+
+    def pair_copy(turn, o):
+        return pltpu.make_async_remote_copy(
+            src_ref=pd.at[1, chunk(o)],
+            dst_ref=pr.at[turn, chunk(o)],
+            send_sem=ysend_sem.at[turn, o],
+            recv_sem=yrecv_sem.at[turn, o],
+            device_id=partner,
+            device_id_type=MESH,
+        )
+
+    def back_copy(turn, o):
+        return pltpu.make_async_remote_copy(
+            src_ref=pd.at[0, chunk(o)],
+            dst_ref=ret.at[turn, chunk(me)],
+            send_sem=bsend_sem.at[turn, o],
+            recv_sem=brecv_sem.at[turn, o],
+            device_id=peer(lax.rem(me - o + slots, slots)),
+            device_id_type=MESH,
+        )
+
+    def add_part(turn, o):
+        pair_copy(turn, o).wait_recv()
+        total = pd[0, chunk(o)].astype(F32) + pr[turn, chunk(o)].astype(F32)
+        return total.astype(BF16)
+
+    def give_back(turn):
+        def body(o):
+            pd[0, chunk(o)] = add_part(turn, o)
+            back_copy(turn, o).start()
+
+        each(1, body)
+        ret[turn, chunk(me)] = add_part(turn, 0)
+
+    def back_end(turn):
+        each(0, lambda o: pair_copy(turn, o).wait_send())
+        each(1, lambda o: back_copy(turn, o).wait_send())
+        each(1, lambda o: back_copy(turn, o).wait_recv())
+
+    def place_online(cols):
+        sx[0, :, cols] = dot(put_any, xo_ref[:, cols]).astype(BF16)
+
+    def place_target(cols):
+        sx[1, :, cols] = dot(put_any, xt_ref[:, cols]).astype(BF16)
+
+    columns(place_online)
+    pl.semaphore_wait(barrier, slots)
+    scatter_start(0, rx.at[0])
+    columns(place_target)
+    scatter_start(1, rx.at[1])
+    for copy in weight_copies:
+        copy.wait()
+    relay(0, rx.at[0])
+    relay(1, rx.at[1])
+
+    def forward(net, part):
+        gate = dot(rx[net, part], wg[net])
+        up = dot(rx[net, part], wu[net])
+        hid[net, part] = (gate * jax.nn.sigmoid(gate) * up).astype(BF16)
+        if net == 0:
+            pre_g[part] = gate
+            pre_u[part] = up
+
+    forward(0, 0)
+    arrived(0, rx.at[0])
+    forward(0, 1)
+    forward(1, 0)
+    arrived(1, rx.at[1])
+    forward(1, 1)
+
+    for part in (1, 0):
+
+        def outputs(cols, part=part):
+            diff = dot(hid[0, part], wd[0, :, cols]) - dot(hid[1, part], wd[1, :, cols])
+            pd[part, :, cols] = diff.astype(BF16)
+
+        columns(outputs)
+        if part == 1:
+            each(0, lambda o: pair_copy(0, o).start())
+    give_back(0)
+    scatter_end(0, rx.at[0])
+    scatter_end(1, rx.at[1])
+    back_end(0)
+
+    p0, p1 = probs_ref[:, 0:1], probs_ref[:, 1:2]
+
+    def cotangents(cols):
+        back = ret[0, :, cols]
+        diff = p0 * dot(take[0], back) + p1 * dot(take[1], back)
+        cot0, cot1 = (p0 * diff).astype(BF16), (p1 * diff).astype(BF16)
+        sx[2, :, cols] = (dot(put[0], cot0) + dot(put[1], cot1)).astype(BF16)
+
+    columns(cotangents)
+    scatter_start(2, rc)
+    relay(2, rc)
+
+    def hidden_back(part):
+        d_hidden = dot(rc[part], wd[0], contract_last)
+        gate, up = pre_g[part], pre_u[part]
+        sig = jax.nn.sigmoid(gate)
+        dgu[0, part] = (d_hidden * up * sig * (1.0 + gate * (1.0 - sig))).astype(BF16)
+        dgu[1, part] = (d_hidden * (gate * sig)).astype(BF16)
+
+    hidden_back(0)
+    arrived(2, rc)
+    hidden_back(1)
+    for part in (1, 0):
+
+        def row_grads(cols, part=part):
+            total = dot(dgu[0, part], wg[0, cols, :], contract_last)
+            total = total + dot(dgu[1, part], wu[0, cols, :], contract_last)
+            pd[part, :, cols] = total.astype(BF16)
+
+        columns(row_grads)
+        if part == 1:
+            each(0, lambda o: pair_copy(1, o).start())
+    give_back(1)
+
+    def weight_grads(cols):
+        for index, target in ((0, gg_ref), (1, gu_ref)):
+            total = dot(rx[0, 0, :, cols], dgu[index, 0], contract_first)
+            total = total + dot(rx[0, 1, :, cols], dgu[index, 1], contract_first)
+            target[cols, :] = total.astype(BF16)
+        total = dot(hid[0, 0], rc[0, :, cols], contract_first)
+        total = total + dot(hid[0, 1], rc[1, :, cols], contract_first)
+        gd_ref[:, cols] = total.astype(BF16)
+
+    columns(weight_grads)
+    scatter_end(2, rc)
+    back_end(1)
+
+    def inputs_grad(cols):
+        ig_ref[:, cols] = dot(take_any, ret[1, :, cols]).astype(BF16)
+
+    columns(inputs_grad)
+
+
+def shards(
+    x_online,
+    x_target,
+    routes,
+    gate_probs,
+    expert_place,
+    gate_online,
+    up_online,
+    down_online,
+    gate_target,
+    up_target,
+    down_target,
+):
+    tok, width = x_online.shape
+    slots = expert_place.shape[0]
+    n_ex = lax.axis_size("expert")
+    cap = 2 * ((2 * tok + slots - 1) // slots)
+    rows = slots * cap
+    half = gate_online.shape[2]
+    if cap % 16 or 2 * slots != lax.axis_size("dp") * n_ex:
+        return shards_plain(
+            x_online,
+            x_target,
+            routes,
+            gate_probs,
+            expert_place,
+            gate_online,
+            up_online,
+            down_online,
+            gate_target,
+            up_target,
+            down_target,
+        )
+    chosen = routes.reshape(-1)
+    onehot = (chosen[:, None] == jnp.arange(slots, dtype=jnp.int32)[None, :]).astype(jnp.int32)
+    before = jnp.cumsum(onehot, axis=0) - onehot
+    flat = jnp.sum((before + cap * expert_place[None, :]) * onehot, axis=1).reshape(tok, 2)
+    vmem = pl.BlockSpec(memory_space=pltpu.VMEM)
+    hbm = pl.BlockSpec(memory_space=pl.ANY)
+    dma = pltpu.SemaphoreType.DMA
+    outs = pl.pallas_call(
+        functools.partial(step_kernel, slots, n_ex, cap),
+        out_shape=(
+            jax.ShapeDtypeStruct((tok, width), BF16),
+            jax.ShapeDtypeStruct((width, half), BF16),
+            jax.ShapeDtypeStruct((width, half), BF16),
+            jax.ShapeDtypeStruct((half, width), BF16),
+        ),
+        in_specs=[vmem] * 5 + [hbm] * 6,
+        out_specs=(vmem,) * 4,
+        scratch_shapes=[
+            pltpu.VMEM((2, width, half), BF16),
+            pltpu.VMEM((2, width, half), BF16),
+            pltpu.VMEM((2, half, width), BF16),
+            pltpu.VMEM((3, rows, width), BF16),
+            pltpu.VMEM((2, 2, rows, width), BF16),
+            pltpu.VMEM((2, rows, width), BF16),
+            pltpu.VMEM((2, rows, width), BF16),
+            pltpu.VMEM((2, rows, width), BF16),
+            pltpu.VMEM((2, rows, width), BF16),
+            pltpu.VMEM((2, rows, half), F32),
+            pltpu.VMEM((2, rows, half), F32),
+            pltpu.VMEM((2, 2, rows, half), BF16),
+            pltpu.VMEM((2, 2, rows, half), BF16),
+            dma((6,)),
+            dma((3, slots)),
+            dma((3, slots)),
+            dma((3, slots)),
+            dma((3, slots)),
+            dma((2, slots)),
+            dma((2, slots)),
+            dma((2, slots)),
+            dma((2, slots)),
+        ],
+        compiler_params=pltpu.CompilerParams(
+            collective_id=0, has_side_effects=True, vmem_limit_bytes=60 * 2**20
+        ),
+    )(
+        flat,
+        flat.T,
+        gate_probs,
+        x_online,
+        x_target,
+        gate_online[0],
+        up_online[0],
+        down_online[0],
+        gate_target[0],
+        up_target[0],
+        down_target[0],
+    )
+    return (outs[0], outs[1][None], outs[2][None], outs[3][None])
+
+
 def solution(mesh):
     in_specs = (
         P(("dp", "expert"), None),

time: 693 us -> 312 us (0.45); the launches traced: 683 us -> 310 us
  waiting for transfers between devices: 406 us -> 0 us
  Pallas kernels: 0 us -> 298 us
  blocking collectives: 109 us -> 0 us
  local copies, waits for them, and re-layouts: 68.1 us -> 10.3 us
  starting transfers between devices: 50 us -> 0 us
  matrix products: 28.4 us -> 0 us
  other arithmetic: 20.7 us -> 0.73 us
    pallas_call x0 -> x1, Pallas kernels: none -> 298 us  [shards(): pl.pallas_call(functools.partial(step_kernel, slots, n_ex, cap), out_shap...]
    ppermute x9 -> x0, waiting for transfers between devices: 211 us -> none  [swapped(): return lax.ppermute(block, axis, route)]
    all_to_all x9 -> x0, waiting for transfers between devices: 195 us -> none  [the longest x1 44.9 us: shards(): lax.all_to_all(lax.all_to_all(out_target.reshape(unit_shape), 'dp', split...]
    all_to_all x3 -> x0, blocking collectives: 109 us -> none  [the longest x1 51.5 us: shards(): lax.all_to_all(lax.all_to_all(to_units(cotangent), 'dp', split_axis=0, co...]
    all_to_all x9 -> x0, starting transfers between devices: 41 us -> none  [the longest x1 6.65 us: shards(): lax.all_to_all(lax.all_to_all(to_units(x_target[owner_token]), 'dp', spli...]
    dot_general x11 -> x0, matrix products: 28.4 us -> none  [the longest x1 6.84 us: shards(): jnp.dot(hidden_target, down_tfull, preferred_element_type=jnp.float32)]
    all_to_all x12 -> x0, local copies, waits for them, and re-layouts: 20 us -> none  [the longest x1 3.24 us: shards(): lax.all_to_all(out_target.reshape(unit_shape), 'dp', split_axis=0, concat...]
    scatter x2 -> x0, local copies, waits for them, and re-layouts: 14.2 us -> none  [to_units(): return blank_rows.at[flat_slot].set(source).reshape(dp_count, expert_coun...]
  transfers between devices with their start and end apart: 18 -> 0, of which waited for: 15 -> 0; matrix products, arithmetic and copies ran while one was open for 8% -> 0% of each run, Pallas kernels for 0% -> 0%
where the time goes in v1:
time: 312 us; the launch traced here: 310 us
  Pallas kernels  298 us (96%)
  local copies, waits for them, and re-layouts  10.3 us (3%)
    pallas_call x1, Pallas kernels, shards(): pl.pallas_call(functools.partial(step_kernel, slots, n_ex, cap), out_shap...  298 us
    unnamed x20, local copies, waits for them, and re-layouts  9.01 us

profile of v1, /device:TPU:0, one launch (start us, length us, event | category | flops | bytes accessed | tf_op | source)
XLA Modules:
  0.0 310.0 jit_solution(1716777616181507197)
XLA Ops:
  0.6 0.0 copy-start.6
  0.6 0.6 copy-done.6
  1.3 0.0 copy-start.4
  1.3 0.7 copy-done.4
  2.0 0.1 copy.17
  2.1 0.1 eq.29
  2.2 0.1 eq.25
  2.4 0.6 reduce-window.6
  3.0 0.2 slice_reduce_fusion
  3.2 0.1 fusion.3
  3.3 0.1 reshape.31.flat_ref
  3.4 0.0 copy-start.3
  3.4 0.6 copy.20
  4.1 0.0 copy-start.5
  4.1 0.7 copy-done.5
  4.8 0.7 copy.21.probs_ref
  5.5 0.0 copy-done.3
  5.5 298.3 %shard_map.138 = (bf16[128,2048]{1,0:T(8,128)(2,1)}, bf16[2048,256]{1,0:T(8,128)(2,1)}, bf16[2048,256]{1,0:T(8,128)(2,1)}, bf16[256,2048]{1,0:T(8,128)(2,1)}) custom-call(s32[128,2]{1,0:T(8,128)} %copy-done.3, s32[2,128]{1,0:T(2,128)} %bitcast.42, f32[128,2]{1,0:T(8,128)} %copy.21.probs_ref, bf16[128,2048]{1,0:T(8,128)(2,1)} %xo_ref.1, ...), custom_call_target="tpu_custom_call" | custom-call | tf_op jit(solution)/shard_map/pallas_call | solution.py:528
  303.9 0.0 copy-start.2
  303.9 2.0 copy.28
  305.8 0.0 copy-done.2
  305.8 0.0 copy-start.1
  305.9 1.0 copy.29
  306.8 0.6 copy-done.1
  307.5 0.0 copy-start
  307.5 1.0 copy.30
  308.4 0.6 copy-done
  309.1 1.0 copy.31
  (4 shorter events, 0.1 us)
Async XLA Ops:
  0.6 0.7 copy-start.6
  1.3 0.7 copy-start.4
  3.4 2.1 copy-start.3
  4.1 0.7 copy-start.5
  303.9 2.0 copy-start.2
  305.8 1.6 copy-start.1
  307.5 1.6 copy-start

commit v2 on v1

--- a/solution.py
+++ b/solution.py
@@ -251,6 +251,18 @@
     me = lax.div(dp * n_ex + ex, 2)
     partner = (dp, ex + 1 - 2 * side)
 
+    planes = n_ex // 2
+    group = slots // planes
+    near, window = slots // 2, 3
+
+    def other(i):
+        mask = lax.rem(i, group) * planes + lax.div(i, group)
+        slot, power = 0, 1
+        while power < slots:
+            bit = lax.rem(lax.rem(lax.div(me, power), 2) + lax.rem(lax.div(mask, power), 2), 2)
+            slot, power = slot + bit * power, 2 * power
+        return slot
+
     def peer(slot):
         unit = 2 * slot + side
         return (lax.div(unit, n_ex), lax.rem(unit, n_ex))
@@ -262,7 +274,7 @@
 
     def greet(o, carry):
         pl.semaphore_signal(
-            barrier, inc=1, device_id=peer(lax.rem(me + o, slots)), device_id_type=MESH
+            barrier, inc=1, device_id=peer(other(o)), device_id_type=MESH
         )
         return carry
 
@@ -302,15 +314,18 @@
 
         lax.fori_loop(0, width // tile, step, 0)
 
-    def each(low, body):
+    def each(low, body, high=slots):
         def step(o, carry):
             body(o)
             return carry
 
-        lax.fori_loop(low, slots, step, 0)
+        lax.fori_loop(low, high, step, 0)
+
+    def each_down(low, body):
+        each(0, lambda o: body(slots - 1 - o), slots - low)
 
     def out_copy(net, dst, o):
-        to = lax.rem(me + o, slots)
+        to = other(o)
         return pltpu.make_async_remote_copy(
             src_ref=sx.at[net, chunk(to)],
             dst_ref=dst.at[0, chunk(o)],
@@ -330,24 +345,42 @@
             device_id_type=MESH,
         )
 
-    def scatter_start(net, dst):
-        each(1, lambda o: out_copy(net, dst, o).start())
+    def start_near(net, dst):
+        each(1, lambda o: out_copy(net, dst, o).start(), near)
         dst[0, 0:cap] = sx[net, chunk(me)]
         fwd_copy(net, dst, 0).start()
 
-    def relay(net, dst):
-        def body(o):
+    def start_far(net, dst):
+        each(near, lambda o: out_copy(net, dst, o).start(), near + window)
+
+    def relay(net, dst, then=None):
+        def pass_on(o):
             out_copy(net, dst, o).wait_recv()
             fwd_copy(net, dst, o).start()
 
-        each(1, body)
+        def far(o):
+            pass_on(o)
+            out_copy(net, dst, o).wait_send()
+            out_copy(net, dst, o + window).start()
+
+        def last(o):
+            pass_on(o)
+            out_copy(net, dst, o).wait_send()
+            if then is not None:
+                out_copy(*then, o - (slots - window - near)).start()
+
+        each(1, pass_on, near)
+        if then is not None:
+            start_near(*then)
+        each(near, far, slots - window)
+        each(slots - window, last)
 
     def arrived(net, dst):
         each(0, lambda o: fwd_copy(net, dst, o).wait_recv())
 
     def scatter_end(net, dst):
         each(0, lambda o: fwd_copy(net, dst, o).wait_send())
-        each(1, lambda o: out_copy(net, dst, o).wait_send())
+        each(1, lambda o: out_copy(net, dst, o).wait_send(), near)
 
     def pair_copy(turn, o):
         return pltpu.make_async_remote_copy(
@@ -365,7 +398,7 @@
             dst_ref=ret.at[turn, chunk(me)],
             send_sem=bsend_sem.at[turn, o],
             recv_sem=brecv_sem.at[turn, o],
-            device_id=peer(lax.rem(me - o + slots, slots)),
+            device_id=peer(other(o)),
             device_id_type=MESH,
         )
 
@@ -379,7 +412,7 @@
             pd[0, chunk(o)] = add_part(turn, o)
             back_copy(turn, o).start()
 
-        each(1, body)
+        each_down(1, body)
         ret[turn, chunk(me)] = add_part(turn, 0)
 
     def back_end(turn):
@@ -395,12 +428,12 @@
 
     columns(place_online)
     pl.semaphore_wait(barrier, slots)
-    scatter_start(0, rx.at[0])
+    start_far(0, rx.at[0])
+    start_near(0, rx.at[0])
     columns(place_target)
-    scatter_start(1, rx.at[1])
     for copy in weight_copies:
         copy.wait()
-    relay(0, rx.at[0])
+    relay(0, rx.at[0], (1, rx.at[1]))
     relay(1, rx.at[1])
 
     def forward(net, part):
@@ -426,7 +459,7 @@
 
         columns(outputs)
         if part == 1:
-            each(0, lambda o: pair_copy(0, o).start())
+            each_down(0, lambda o: pair_copy(0, o).start())
     give_back(0)
     scatter_end(0, rx.at[0])
     scatter_end(1, rx.at[1])
@@ -441,7 +474,8 @@
         sx[2, :, cols] = (dot(put[0], cot0) + dot(put[1], cot1)).astype(BF16)
 
     columns(cotangents)
-    scatter_start(2, rc)
+    start_far(2, rc)
+    start_near(2, rc)
     relay(2, rc)
 
     def hidden_back(part):
@@ -463,7 +497,7 @@
 
         columns(row_grads)
         if part == 1:
-            each(0, lambda o: pair_copy(1, o).start())
+            each_down(0, lambda o: pair_copy(1, o).start())
     give_back(1)
 
     def weight_grads(cols):
@@ -504,7 +538,9 @@
     cap = 2 * ((2 * tok + slots - 1) // slots)
     rows = slots * cap
     half = gate_online.shape[2]
-    if cap % 16 or 2 * slots != lax.axis_size("dp") * n_ex:
+    paired = 2 * slots == lax.axis_size("dp") * n_ex and n_ex % 2 == 0
+    halving = slots & (slots - 1) == 0 and n_ex & (n_ex - 1) == 0
+    if cap % 16 or slots < 8 or not (paired and halving):
         return shards_plain(
             x_online,
             x_target,

time: 312 us -> 301 us (0.965)
  Pallas kernels: 298 us -> 289 us
    pallas_call x1, Pallas kernels: 298 us -> 289 us  [shards(): pl.pallas_call(functools.partial(step_kernel, slots, n_ex, cap), out_shap...]
where the time goes in v2:
time: 301 us
  Pallas kernels  289 us (96%)
  local copies, waits for them, and re-layouts  10.3 us (3%)
    pallas_call x1, Pallas kernels, shards(): pl.pallas_call(functools.partial(step_kernel, slots, n_ex, cap), out_shap...  289 us
    unnamed x20, local copies, waits for them, and re-layouts  9.01 us

profile of v2, /device:TPU:0, one launch (start us, length us, event | category | flops | bytes accessed | tf_op | source)
XLA Modules:
  0.0 301.1 jit_solution(10309349987638792709)
XLA Ops:
  0.6 0.0 copy-start.6
  0.6 0.6 copy-done.6
  1.3 0.0 copy-start.4
  1.3 0.7 copy-done.4
  2.0 0.1 copy.17
  2.1 0.1 eq.29
  2.2 0.1 eq.25
  2.4 0.6 reduce-window.6
  3.0 0.2 slice_reduce_fusion
  3.2 0.1 fusion.3
  3.3 0.1 reshape.31.flat_ref
  3.4 0.0 copy-start.3
  3.4 0.6 copy.20
  4.1 0.0 copy-start.5
  4.1 0.7 copy-done.5
  4.8 0.7 copy.21.probs_ref
  5.5 0.0 copy-done.3
  5.5 289.4 %shard_map.138 = (bf16[128,2048]{1,0:T(8,128)(2,1)}, bf16[2048,256]{1,0:T(8,128)(2,1)}, bf16[2048,256]{1,0:T(8,128)(2,1)}, bf16[256,2048]{1,0:T(8,128)(2,1)}) custom-call(s32[128,2]{1,0:T(8,128)} %copy-done.3, s32[2,128]{1,0:T(2,128)} %bitcast.42, f32[128,2]{1,0:T(8,128)} %copy.21.probs_ref, bf16[128,2048]{1,0:T(8,128)(2,1)} %xo_ref.1, ...), custom_call_target="tpu_custom_call" | custom-call | tf_op jit(solution)/shard_map/pallas_call | solution.py:564
  294.9 0.0 copy-start.2
  294.9 2.0 copy.28
  296.9 0.0 copy-done.2
  296.9 0.0 copy-start.1
  296.9 1.0 copy.29
  297.9 0.6 copy-done.1
  298.5 0.0 copy-start
  298.5 1.0 copy.30
  299.5 0.6 copy-done
  300.1 1.0 copy.31
  (4 shorter events, 0.1 us)
Async XLA Ops:
  0.6 0.7 copy-start.6
  1.3 0.7 copy-start.4
  3.4 2.1 copy-start.3
  4.1 0.7 copy-start.5
  294.9 2.0 copy-start.2
  296.9 1.6 copy-start.1
  298.5 1.6 copy-start

commit v3 on v2

--- a/solution.py
+++ b/solution.py
@@ -253,7 +253,7 @@
 
     planes = n_ex // 2
     group = slots // planes
-    near, window = slots // 2, 3
+    near, window = slots // 2, 5
 
     def other(i):
         mask = lax.rem(i, group) * planes + lax.div(i, group)
@@ -307,12 +307,18 @@
     take = [one_hot(col_iota == flat_ref[:, k : k + 1]) for k in range(2)]
     take_any = one_hot((col_iota == flat_ref[:, 0:1]) | (col_iota == flat_ref[:, 1:2]))
 
-    def columns(body):
+    def columns(body, low=0, high=width):
         def step(i, carry):
             body(pl.ds(pl.multiple_of(i * tile, tile), tile))
             return carry
 
-        lax.fori_loop(0, width // tile, step, 0)
+        lax.fori_loop(low // tile, high // tile, step, 0)
+
+    middle = width // 2
+    span = [(0, middle), (middle, width)]
+
+    def part_of(net):
+        return pl.ds(*(((net % 2) * middle, middle) if net >= 2 else (0, width)))
 
     def each(low, body, high=slots):
         def step(o, carry):
@@ -327,8 +333,8 @@
     def out_copy(net, dst, o):
         to = other(o)
         return pltpu.make_async_remote_copy(
-            src_ref=sx.at[net, chunk(to)],
-            dst_ref=dst.at[0, chunk(o)],
+            src_ref=sx.at[min(net, 2), chunk(to), part_of(net)],
+            dst_ref=dst.at[0, chunk(o), part_of(net)],
             send_sem=send_sem.at[net, o],
             recv_sem=recv_sem.at[net, o],
             device_id=peer(to),
@@ -337,8 +343,8 @@
 
     def fwd_copy(net, dst, o):
         return pltpu.make_async_remote_copy(
-            src_ref=dst.at[0, chunk(o)],
-            dst_ref=dst.at[1, chunk(o)],
+            src_ref=dst.at[0, chunk(o), part_of(net)],
+            dst_ref=dst.at[1, chunk(o), part_of(net)],
             send_sem=fsend_sem.at[net, o],
             recv_sem=frecv_sem.at[net, o],
             device_id=partner,
@@ -347,7 +353,7 @@
 
     def start_near(net, dst):
         each(1, lambda o: out_copy(net, dst, o).start(), near)
-        dst[0, 0:cap] = sx[net, chunk(me)]
+        dst[0, 0:cap, part_of(net)] = sx[min(net, 2), chunk(me), part_of(net)]
         fwd_copy(net, dst, 0).start()
 
     def start_far(net, dst):
@@ -382,10 +388,13 @@
         each(0, lambda o: fwd_copy(net, dst, o).wait_send())
         each(1, lambda o: out_copy(net, dst, o).wait_send(), near)
 
+    def half_of(turn):
+        return pl.ds((turn % 2) * middle, middle)
+
     def pair_copy(turn, o):
         return pltpu.make_async_remote_copy(
-            src_ref=pd.at[1, chunk(o)],
-            dst_ref=pr.at[turn, chunk(o)],
+            src_ref=pd.at[1, chunk(o), half_of(turn)],
+            dst_ref=pr.at[turn // 2, chunk(o), half_of(turn)],
             send_sem=ysend_sem.at[turn, o],
             recv_sem=yrecv_sem.at[turn, o],
             device_id=partner,
@@ -394,8 +403,8 @@
 
     def back_copy(turn, o):
         return pltpu.make_async_remote_copy(
-            src_ref=pd.at[0, chunk(o)],
-            dst_ref=ret.at[turn, chunk(me)],
+            src_ref=pd.at[0, chunk(o), half_of(turn)],
+            dst_ref=ret.at[turn // 2, chunk(me), half_of(turn)],
             send_sem=bsend_sem.at[turn, o],
             recv_sem=brecv_sem.at[turn, o],
             device_id=peer(other(o)),
@@ -404,20 +413,23 @@
 
     def add_part(turn, o):
         pair_copy(turn, o).wait_recv()
-        total = pd[0, chunk(o)].astype(F32) + pr[turn, chunk(o)].astype(F32)
+        cols = half_of(turn)
+        total = pd[0, chunk(o), cols].astype(F32) + pr[turn // 2, chunk(o), cols].astype(F32)
         return total.astype(BF16)
 
     def give_back(turn):
         def body(o):
-            pd[0, chunk(o)] = add_part(turn, o)
+            pd[0, chunk(o), half_of(turn)] = add_part(turn, o)
             back_copy(turn, o).start()
 
         each_down(1, body)
-        ret[turn, chunk(me)] = add_part(turn, 0)
-
-    def back_end(turn):
+        ret[turn // 2, chunk(me), half_of(turn)] = add_part(turn, 0)
+
+    def back_sent(turn):
         each(0, lambda o: pair_copy(turn, o).wait_send())
         each(1, lambda o: back_copy(turn, o).wait_send())
+
+    def back_came(turn):
         each(1, lambda o: back_copy(turn, o).wait_recv())
 
     def place_online(cols):
@@ -451,19 +463,18 @@
     arrived(1, rx.at[1])
     forward(1, 1)
 
-    for part in (1, 0):
-
-        def outputs(cols, part=part):
+    for side_part in (1, 0):
+
+        def outputs(cols, part=side_part):
             diff = dot(hid[0, part], wd[0, :, cols]) - dot(hid[1, part], wd[1, :, cols])
             pd[part, :, cols] = diff.astype(BF16)
 
-        columns(outputs)
-        if part == 1:
-            each_down(0, lambda o: pair_copy(0, o).start())
+        for turn in (0, 1):
+            columns(outputs, *span[turn])
+            if side_part == 1:
+                each_down(0, lambda o, turn=turn: pair_copy(turn, o).start())
     give_back(0)
-    scatter_end(0, rx.at[0])
-    scatter_end(1, rx.at[1])
-    back_end(0)
+    give_back(1)
 
     p0, p1 = probs_ref[:, 0:1], probs_ref[:, 1:2]
 
@@ -473,10 +484,18 @@
         cot0, cot1 = (p0 * diff).astype(BF16), (p1 * diff).astype(BF16)
         sx[2, :, cols] = (dot(put[0], cot0) + dot(put[1], cot1)).astype(BF16)
 
-    columns(cotangents)
+    back_came(0)
+    columns(cotangents, *span[0])
     start_far(2, rc)
     start_near(2, rc)
-    relay(2, rc)
+    back_came(1)
+    columns(cotangents, *span[1])
+    relay(2, rc, (3, rc))
+    relay(3, rc)
+    scatter_end(0, rx.at[0])
+    scatter_end(1, rx.at[1])
+    back_sent(0)
+    back_sent(1)
 
     def hidden_back(part):
         d_hidden = dot(rc[part], wd[0], contract_last)
@@ -487,18 +506,21 @@
 
     hidden_back(0)
     arrived(2, rc)
+    arrived(3, rc)
     hidden_back(1)
-    for part in (1, 0):
-
-        def row_grads(cols, part=part):
+    for side_part in (1, 0):
+
+        def row_grads(cols, part=side_part):
             total = dot(dgu[0, part], wg[0, cols, :], contract_last)
             total = total + dot(dgu[1, part], wu[0, cols, :], contract_last)
             pd[part, :, cols] = total.astype(BF16)
 
-        columns(row_grads)
-        if part == 1:
-            each_down(0, lambda o: pair_copy(1, o).start())
-    give_back(1)
+        for turn in (2, 3):
+            columns(row_grads, *span[turn - 2])
+            if side_part == 1:
+                each_down(0, lambda o, turn=turn: pair_copy(turn, o).start())
+    give_back(2)
+    give_back(3)
 
     def weight_grads(cols):
         for index, target in ((0, gg_ref), (1, gu_ref)):
@@ -511,12 +533,17 @@
 
     columns(weight_grads)
     scatter_end(2, rc)
-    back_end(1)
+    scatter_end(3, rc)
+    back_came(2)
 
     def inputs_grad(cols):
         ig_ref[:, cols] = dot(take_any, ret[1, :, cols]).astype(BF16)
 
-    columns(inputs_grad)
+    columns(inputs_grad, *span[0])
+    back_came(3)
+    columns(inputs_grad, *span[1])
+    back_sent(2)
+    back_sent(3)
 
 
 def shards(
@@ -540,7 +567,7 @@
     half = gate_online.shape[2]
     paired = 2 * slots == lax.axis_size("dp") * n_ex and n_ex % 2 == 0
     halving = slots & (slots - 1) == 0 and n_ex & (n_ex - 1) == 0
-    if cap % 16 or slots < 8 or not (paired and halving):
+    if cap % 16 or width % 1024 or slots < 16 or not (paired and halving):
         return shards_plain(
             x_online,
             x_target,
@@ -586,14 +613,14 @@
             pltpu.VMEM((2, 2, rows, half), BF16),
             pltpu.VMEM((2, 2, rows, half), BF16),
             dma((6,)),
-            dma((3, slots)),
-            dma((3, slots)),
-            dma((3, slots)),
-            dma((3, slots)),
-            dma((2, slots)),
-            dma((2, slots)),
-            dma((2, slots)),
-            dma((2, slots)),
+            dma((4, slots)),
+            dma((4, slots)),
+            dma((4, slots)),
+            dma((4, slots)),
+            dma((4, slots)),
+            dma((4, slots)),
+            dma((4, slots)),
+            dma((4, slots)),
         ],
         compiler_params=pltpu.CompilerParams(
             collective_id=0, has_side_effects=True, vmem_limit_bytes=60 * 2**20

time: 301 us -> 285 us (0.947)
  Pallas kernels: 289 us -> 273 us
    pallas_call x1, Pallas kernels: 289 us -> 273 us  [shards(): pl.pallas_call(functools.partial(step_kernel, slots, n_ex, cap), out_shap...]
where the time goes in v3:
time: 285 us
  Pallas kernels  273 us (96%)
  local copies, waits for them, and re-layouts  10.3 us (4%)
    pallas_call x1, Pallas kernels, shards(): pl.pallas_call(functools.partial(step_kernel, slots, n_ex, cap), out_shap...  273 us
    unnamed x20, local copies, waits for them, and re-layouts  9.01 us

profile of v3, /device:TPU:0, one launch (start us, length us, event | category | flops | bytes accessed | tf_op | source)
XLA Modules:
  0.0 284.6 jit_solution(14891896521282774414)
XLA Ops:
  0.6 0.0 copy-start.6
  0.6 0.6 copy-done.6
  1.3 0.0 copy-start.4
  1.3 0.7 copy-done.4
  2.0 0.1 copy.17
  2.1 0.1 eq.29
  2.2 0.1 eq.25
  2.4 0.6 reduce-window.6
  3.0 0.2 slice_reduce_fusion
  3.2 0.1 fusion.3
  3.3 0.1 reshape.31.flat_ref
  3.4 0.0 copy-start.3
  3.4 0.6 copy.20
  4.1 0.0 copy-start.5
  4.1 0.7 copy-done.5
  4.8 0.7 copy.21.probs_ref
  5.5 0.0 copy-done.3
  5.5 272.9 %shard_map.138 = (bf16[128,2048]{1,0:T(8,128)(2,1)}, bf16[2048,256]{1,0:T(8,128)(2,1)}, bf16[2048,256]{1,0:T(8,128)(2,1)}, bf16[256,2048]{1,0:T(8,128)(2,1)}) custom-call(s32[128,2]{1,0:T(8,128)} %copy-done.3, s32[2,128]{1,0:T(2,128)} %bitcast.42, f32[128,2]{1,0:T(8,128)} %copy.21.probs_ref, bf16[128,2048]{1,0:T(8,128)(2,1)} %xo_ref.1, ...), custom_call_target="tpu_custom_call" | custom-call | tf_op jit(solution)/shard_map/pallas_call | solution.py:591
  278.4 0.0 copy-start.2
  278.4 2.0 copy.28
  280.4 0.0 copy-done.2
  280.4 0.0 copy-start.1
  280.4 1.0 copy.29
  281.4 0.6 copy-done.1
  282.0 0.0 copy-start
  282.0 1.0 copy.30
  283.0 0.6 copy-done
  283.6 1.0 copy.31
  (4 shorter events, 0.1 us)
Async XLA Ops:
  0.6 0.7 copy-start.6
  1.3 0.7 copy-start.4
  3.4 2.1 copy-start.3
  4.1 0.7 copy-start.5
  278.4 2.0 copy-start.2
  280.4 1.6 copy-start.1
  282.0 1.6 copy-start
